TPU v7x, 256 devices: a whole 4x4x8 slice. The times are simulated.
256 devices in a mesh: row: 32 (over z_lo, x, core), col: 8 (over z_hi, y).
Axes of the slice: x: 4, y: 4, z: 8 (z_hi: 2, z_lo: 4; z = z_hi * 4 + z_lo), core: 2. Of those that a mesh axis runs over, the one named last changes fastest.
Arguments:
- pair: bfloat16 [512, 512, 128], P('row', 'col'), may hold values from -6 to 6
- cotangent: bfloat16 [64, 512, 512], P(None, 'row', 'col'), may hold values from -0.59765625 to 0.59765625
- w_left: bfloat16 [128, 64], replicated, may hold values from -0.5 to 0.5
- w_left_gate: bfloat16 [128, 64], replicated, may hold values from -0.5 to 0.5
- w_right: bfloat16 [128, 64], replicated, may hold values from -0.5 to 0.5
- w_right_gate: bfloat16 [128, 64], replicated, may hold values from -0.5 to 0.5
Outputs:
- pair_gradient: bfloat16 [512, 512, 128], P('row', 'col')
- grad_left: float32 [128, 64], replicated
- grad_left_gate: float32 [128, 64], replicated
- grad_right: float32 [128, 64], replicated
- grad_right_gate: float32 [128, 64], replicated
All inputs are finite; a program needn't handle non-finite values.
Results may differ from a plain program's by a relative error of at most 0.0082.
Values may be sent and summed in bfloat16 or wider, within the bound.
A program may use at most 64 MiB of HBM per device.

v0:
```python
import jax
import jax.numpy as jnp
from jax import lax
from jax.sharding import PartitionSpec as P


def shards(pair, cotangent, w_left, w_left_gate, w_right, w_right_gate):
    pair_f = pair.astype(jnp.float32)
    average = jnp.mean(pair_f, axis=-1, keepdims=True)
    centered_input = pair_f - average
    variance = jnp.mean(centered_input * centered_input, axis=-1, keepdims=True)
    inverse_scale = 1.0 / jnp.sqrt(variance + 1e-05)
    standardized_input = centered_input * inverse_scale
    normalized_input = standardized_input.astype(jnp.bfloat16)
    stacked = jnp.concatenate([w_left, w_left_gate, w_right, w_right_gate], axis=1)
    projected = jnp.einsum(
        "rcd,dh->hrc", normalized_input, stacked, preferred_element_type=jnp.float32
    )
    q_left, p_left, q_right, p_right = jnp.split(projected, 4, axis=0)
    s_left = jax.nn.sigmoid(p_left)
    s_right = jax.nn.sigmoid(p_right)
    left = (s_left * q_left).astype(jnp.bfloat16)
    right = (s_right * q_right).astype(jnp.bfloat16)
    g_chan, left_chan, right_chan = (
        lax.all_to_all(cotangent, "col", split_axis=0, concat_axis=2, tiled=True),
        lax.all_to_all(left, "col", split_axis=0, concat_axis=2, tiled=True),
        lax.all_to_all(right, "col", split_axis=0, concat_axis=2, tiled=True),
    )
    residues = g_chan.shape[2]
    col_block = g_chan
    d_left = jnp.einsum(
        "hij,hjk->hik",
        col_block,
        lax.all_gather(right_chan, "row", axis=1, tiled=True),
        preferred_element_type=jnp.float32,
    )
    col_block = g_chan
    summed = lax.psum_scatter(
        jnp.einsum("hij,hik->jhk", col_block, left_chan, preferred_element_type=jnp.float32),
        "row",
        scatter_dimension=0,
        tiled=True,
    )
    d_right = jnp.transpose(summed, (1, 0, 2))
    d_left_tile, d_right_tile = (
        lax.all_to_all(d_left.astype(jnp.bfloat16), "col", split_axis=2, concat_axis=0, tiled=True),
        lax.all_to_all(
            d_right.astype(jnp.bfloat16), "col", split_axis=2, concat_axis=0, tiled=True
        ),
    )
    grad_l = d_left_tile.astype(jnp.float32)
    grad_r = d_right_tile.astype(jnp.float32)
    e_left = grad_l * s_left
    f_left = grad_l * q_left * s_left * (1.0 - s_left)
    e_right = grad_r * s_right
    f_right = grad_r * q_right * s_right * (1.0 - s_right)
    grads = jnp.concatenate([e_left, f_left, e_right, f_right], axis=0).astype(jnp.bfloat16)
    local_weights = jnp.einsum(
        "rcd,hrc->dh", normalized_input, grads, preferred_element_type=jnp.float32
    )
    total_weights = lax.psum(local_weights, ("row", "col")) / residues
    normalized_gradient = jnp.einsum(
        "hrc,dh->rcd", grads, stacked, preferred_element_type=jnp.float32
    )
    gradient_mean = jnp.mean(normalized_gradient, axis=-1, keepdims=True)
    gradient_input_mean = jnp.mean(normalized_gradient * standardized_input, axis=-1, keepdims=True)
    pair_gradient = (
        (normalized_gradient - gradient_mean - standardized_input * gradient_input_mean)
        * inverse_scale
    ).astype(jnp.bfloat16)
    pieces_w = jnp.split(total_weights, 4, axis=1)
    return (pair_gradient, pieces_w[0], pieces_w[1], pieces_w[2], pieces_w[3])


def solution(mesh):
    in_specs = (P("row", "col", None), P(None, "row", "col"), P(), P(), P(), P())
    out_specs = (P("row", "col", None), P(), P(), P(), P())
    return jax.shard_map(shards, mesh=mesh, in_specs=in_specs, out_specs=out_specs, check_vma=False)
```

profile of v0, /device:TPU:2, one launch (start us, length us, event | category | flops | bytes accessed | tf_op | source)
XLA Modules:
  0.0 579.7 jit_solution(9537658770375944991)
XLA Ops:
  7.2 1.2 convert_reduce_fusion
  8.4 1.3 fusion.10
  9.8 0.8 copy.87
  10.6 0.8 copy.88
  11.4 0.8 copy.89
  12.3 0.8 copy.90
  13.1 1.4 fusion.18
  15.3 21.4 %all_to_all.72 = bf16[8,2,4096]{2,1,0:T(2,128)(2,1)S(1)} all-to-all(bf16[8,2,4096]{2,1,0:T(2,128)(2,1)S(1)} %reshape.47), channel_id=1, replica_groups=mesh['row'=32,'col'=8] {'col'}, dimensions={0} | all-to-all | bytes 262144 | tf_op jit(solution)/shard_map/all_to_all | solution.py:27
  37.1 0.9 all_to_all.56
  38.3 13.0 %all_to_all.73 = bf16[8,2,4096]{2,1,0:T(2,128)(2,1)S(1)} all-to-all(bf16[8,2,4096]{2,1,0:T(2,128)(2,1)S(1)} %reshape.45), channel_id=1, replica_groups=mesh['row'=32,'col'=8] {'col'}, dimensions={0} | all-to-all | bytes 262144 | tf_op jit(solution)/shard_map/all_to_all | solution.py:25
  51.9 43.9 %all-gather.2.cloned.1.call-done = bf16[8,512,512]{2,1,0:T(8,128)(2,1)} async-done(((bf16[8,16,512]{2,1,0:T(8,128)(2,1)}), bf16[8,512,512]{2,1,0:T(8,128)(2,1)}) %all-gather.2.cloned.1.call-update) | async-done | bytes 4194320 | tf_op jit(solution)/shard_map/all_gather | solution.py:34
  95.9 2.8 fusion
  98.7 0.8 copy.94
  99.5 1.1 reshape.49
  100.5 18.0 %all_to_all.74 = bf16[8,2,4096]{2,1,0:T(2,128)(2,1)S(1)} all-to-all(bf16[8,2,4096]{2,1,0:T(2,128)(2,1)S(1)} %reshape.49), channel_id=1, replica_groups=mesh['row'=32,'col'=8] {'col'}, dimensions={0} | all-to-all | bytes 262144 | tf_op jit(solution)/shard_map/all_to_all | solution.py:46
  118.6 0.7 reshape.50
  119.3 0.7 copy.95
  121.4 13.0 %all_to_all.75 = bf16[8,2,4096]{2,1,0:T(2,128)(2,1)S(1)} all-to-all(bf16[8,2,4096]{2,1,0:T(2,128)(2,1)S(1)} %reshape.51), channel_id=1, replica_groups=mesh['row'=32,'col'=8] {'col'}, dimensions={0} | all-to-all | bytes 262144 | tf_op jit(solution)/shard_map/all_to_all | solution.py:26
  135.1 4.5 convolution_bitcast_fusion
  139.6 10.4 %copy.101 = f32[512,8,512]{2,1,0:T(8,128)} copy(f32[512,8,512]{0,2,1:T(8,128)} %convolution_bitcast_fusion) | data formatting | bytes 16777216 | tf_op jit(solution)/shard_map/hij,hik->jhk/transpose | solution.py:39
  150.1 150.5 %reduce-scatter.2.cloned.1.call-done = f32[16,8,512]{2,1,0:T(8,128)} async-done(((f32[512,8,512]{2,1,0:T(8,128)}), f32[16,8,512]{2,1,0:T(8,128)}) %reduce-scatter.2.cloned.1.call-update) | async-done | bytes 262160 | tf_op jit(solution)/shard_map/reduce_scatter | solution.py:38
  300.5 1.0 convert_bitcast_fusion
  301.5 0.8 copy.102
  302.3 1.1 reshape.53
  303.4 16.3 %all_to_all.76 = bf16[8,2,4096]{2,1,0:T(2,128)(2,1)S(1)} all-to-all(bf16[8,2,4096]{2,1,0:T(2,128)(2,1)S(1)} %reshape.53), channel_id=1, replica_groups=mesh['row'=32,'col'=8] {'col'}, dimensions={0} | all-to-all | bytes 262144 | tf_op jit(solution)/shard_map/all_to_all | solution.py:47
  320.4 0.7 copy.103
  322.0 1.5 convolution_bitcast_fusion.1
  323.5 1.0 fusion.21
  324.5 1.3 fusion.9
  325.9 243.5 %all-reduce.2.cloned.1.call-done = f32[128,256]{1,0:T(8,128)} async-done(((f32[128,256]{1,0:T(8,128)}), f32[128,256]{1,0:T(8,128)}) %all-reduce.2.cloned.1.call-update) | async-done | bytes 131088 | tf_op jit(solution)/shard_map/psum | solution.py:61
  569.4 0.9 broadcast_multiply_fusion
  570.4 0.7 copy.110
  (40 shorter events, 7.8 us)
Async XLA Ops:
  7.2 30.9 %copy-start.1 = (bf16[64,16,64]{2,1,0:T(8,128)(2,1)S(1)}, bf16[64,16,64]{2,1,0:T(8,128)(2,1)}, u32[]{:S(2)}) copy-start(bf16[64,16,64]{2,1,0:T(8,128)(2,1)} %param.7) | copy-start | bytes 393220
  7.2 88.7 %all-gather.2.cloned.1.call-start = ((), (), s32[]{:S(2)}) async-start(), calls=%async_computation.6 | async-start | bytes 4325376 | tf_op jit(solution)/shard_map/all_gather | solution.py:34
  38.0 262.5 %reduce-scatter.2.cloned.1.call-start = ((), (), s32[]{:S(2)}) async-start(), calls=%async_computation.7 | async-start | bytes 8650752 | tf_op jit(solution)/shard_map/reduce_scatter | solution.py:38
  150.0 419.4 %all-reduce.2.cloned.1.call-start = ((), (), s32[]{:S(2)}) async-start(), calls=%async_computation.8 | async-start | bytes 262144 | tf_op jit(solution)/shard_map/psum | solution.py:61
  302.3 19.7 %copy-start = (bf16[16,64,128]{2,1,0:T(8,128)(2,1)S(1)}, bf16[16,64,128]{2,1,0:T(8,128)(2,1)}, u32[]{:S(2)}) copy-start(bf16[16,64,128]{2,1,0:T(8,128)(2,1)} %param.6) | copy-start | bytes 786436
Sparse Core Ops, SparseCore 0:
  38.1 57.7 all-gather.1
  150.1 150.3 reduce-scatter.1
  324.7 244.7 all-reduce.1
where the time goes:
time: 581 us; the launch traced here: 580 us
  waiting for transfers between devices  438 us (75%)
  blocking collectives  81.8 us (14%)
  local copies, waits for them, and re-layouts  27.9 us (5%)
  between operations  14 us (2%)
  matrix products  11.3 us (2%)
  other arithmetic  6.66 us (1%)
    psum x1, waiting for transfers between devices, shards(): total_weights = lax.psum(local_weights, ('row', 'col')) / residues  244 us
    reduce_scatter x1, waiting for transfers between devices, shards(): lax.psum_scatter(jnp.einsum('hij,hik->jhk', col_block, left_chan, preferr...  150 us
    all_gather x1, waiting for transfers between devices, shards(): lax.all_gather(right_chan, 'row', axis=1, tiled=True)  43.9 us
    all_to_all x1, blocking collectives, shards(): lax.all_to_all(right, 'col', split_axis=0, concat_axis=2, tiled=True)  21.4 us
    all_to_all x1, blocking collectives, shards(): lax.all_to_all(d_left.astype(jnp.bfloat16), 'col', split_axis=2, concat_a...  18 us
    all_to_all x1, blocking collectives, shards(): lax.all_to_all(d_right.astype(jnp.bfloat16), 'col', split_axis=2, concat_...  16.3 us
    all_to_all x1, blocking collectives, shards(): lax.all_to_all(left, 'col', split_axis=0, concat_axis=2, tiled=True)  13 us
    all_to_all x1, blocking collectives, shards(): lax.all_to_all(cotangent, 'col', split_axis=0, concat_axis=2, tiled=True)  13 us
  transfers between devices with their start and end apart: 3, of which 3 were waited for; matrix products, arithmetic and copies ran while one was open for 0% of the time, Pallas kernels for 0%

commit v1 on v0

--- a/solution.py
+++ b/solution.py
@@ -2,6 +2,11 @@
 import jax.numpy as jnp
 from jax import lax
 from jax.sharding import PartitionSpec as P
+
+
+def gather_over(x, axis, dim):
+    sent = jnp.stack([x] * lax.axis_size(axis))
+    return jnp.concatenate(lax.all_to_all(sent, axis, 0, 0), axis=dim)
 
 
 def shards(pair, cotangent, w_left, w_left_gate, w_right, w_right_gate):
@@ -31,7 +36,7 @@
     d_left = jnp.einsum(
         "hij,hjk->hik",
         col_block,
-        lax.all_gather(right_chan, "row", axis=1, tiled=True),
+        gather_over(right_chan, "row", 1),
         preferred_element_type=jnp.float32,
     )
     col_block = g_chan

time: 581 us -> 633 us (1.090)
  waiting for transfers between devices: 438 us -> 505 us
  blocking collectives: 81.8 us -> 42.1 us
  starting transfers between devices: 0.12 us -> 21.1 us
    all_to_all x0 -> x3, waiting for transfers between devices: none -> 112 us  [the longest x1 92.7 us: gather_over(): return jnp.concatenate(lax.all_to_all(sent, axis, 0, 0), axis=dim)]
    all_gather x1 -> x0, waiting for transfers between devices: 43.9 us -> none  [shards(): lax.all_gather(right_chan, 'row', axis=1, tiled=True)]
    all_to_all x2 -> x0, blocking collectives: 34.4 us -> none  [the longest x1 21.4 us: shards(): lax.all_to_all(right, 'col', split_axis=0, concat_axis=2, tiled=True)]
    all_to_all x0 -> x3, starting transfers between devices: none -> 20.9 us  [the longest x1 11.1 us: shards(): lax.all_to_all(right, 'col', split_axis=0, concat_axis=2, tiled=True)]
  transfers between devices with their start and end apart: 3 -> 5, of which waited for: 3 -> 5; matrix products, arithmetic and copies ran while one was open for 0% -> 1% of each run, Pallas kernels for 0% -> 0%
where the time goes in v1:
time: 633 us; the launch traced here: 632 us
  waiting for transfers between devices  505 us (80%)
  blocking collectives  42.1 us (7%)
  local copies, waits for them, and re-layouts  33.7 us (5%)
  starting transfers between devices  21.1 us (3%)
  between operations  14.3 us (2%)
  matrix products  9.11 us (1%)
  other arithmetic  6.67 us (1%)
    psum x1, waiting for transfers between devices, shards(): total_weights = lax.psum(local_weights, ('row', 'col')) / residues  243 us
    reduce_scatter x1, waiting for transfers between devices, shards(): lax.psum_scatter(jnp.einsum('hij,hik->jhk', col_block, left_chan, preferr...  150 us
    all_to_all x1, waiting for transfers between devices, gather_over(): return jnp.concatenate(lax.all_to_all(sent, axis, 0, 0), axis=dim)  92.7 us
    all_to_all x1, blocking collectives, shards(): lax.all_to_all(d_right.astype(jnp.bfloat16), 'col', split_axis=2, concat_...  16 us
    all_to_all x1, blocking collectives, shards(): lax.all_to_all(left, 'col', split_axis=0, concat_axis=2, tiled=True)  13.1 us
    all_to_all x1, blocking collectives, shards(): lax.all_to_all(d_left.astype(jnp.bfloat16), 'col', split_axis=2, concat_a...  13 us
  transfers between devices with their start and end apart: 5, of which 5 were waited for; matrix products, arithmetic and copies ran while one was open for 1% of the time, Pallas kernels for 0%

profile of v1, /device:TPU:2, one launch (start us, length us, event | category | flops | bytes accessed | tf_op | source)
XLA Modules:
  0.0 632.1 jit_solution(1455483045885680434)
XLA Ops:
  7.2 1.2 convert_reduce_fusion
  8.4 1.3 fusion.10
  9.7 0.8 copy.88
  10.6 0.8 copy.89
  11.4 0.8 copy.90
  12.2 0.8 copy.91
  13.1 1.4 fusion.18
  15.0 0.9 reshape.58
  15.9 11.1 %all-to-all-start = ((bf16[8,2,4096]{2,1,0:T(2,128)(2,1)}), bf16[8,2,4096]{2,1,0:T(2,128)(2,1)S(1)}, u32[]{:S(2)}, u32[]{:S(2)}) async-start(bf16[8,2,4096]{2,1,0:T(2,128)(2,1)} %reshape.58), calls=%async_computation | async-start | bytes 262144 | tf_op jit(solution)/shard_map/all_to_all | solution.py:32
  27.0 0.9 reshape.56
  27.9 9.6 %all-to-all-done = bf16[8,2,4096]{2,1,0:T(2,128)(2,1)S(1)} async-done(((bf16[8,2,4096]{2,1,0:T(2,128)(2,1)}), bf16[8,2,4096]{2,1,0:T(2,128)(2,1)S(1)}, u32[]{:S(2)}, u32[]{:S(2)}) %all-to-all-start) | async-done | bytes 131104 | tf_op jit(solution)/shard_map/all_to_all | solution.py:32
  37.5 3.4 all-to-all-start.2
  41.5 9.8 %all-to-all-done.2 = bf16[8,2,4096]{2,1,0:T(2,128)(2,1)S(1)} async-done(((bf16[8,2,4096]{2,1,0:T(2,128)(2,1)}), bf16[8,2,4096]{2,1,0:T(2,128)(2,1)S(1)}, u32[]{:S(2)}, u32[]{:S(2)}) %all-to-all-start.2) | async-done | bytes 131104 | tf_op jit(solution)/shard_map/all_to_all | solution.py:30
  51.3 2.5 stack.5
  53.8 6.4 %all-to-all-start.1 = ((bf16[32,8,16,512]{3,2,1,0:T(8,128)(2,1)}), bf16[32,8,16,512]{3,2,1,0:T(8,128)(2,1)}, u32[]{:S(2)}, u32[]{:S(2)}) async-start(bf16[32,8,16,512]{3,2,1,0:T(8,128)(2,1)} %stack.5), calls=%async_computation.1 | async-start | bytes 8388608 | tf_op jit(solution)/shard_map/all_to_all | solution.py:9
  60.9 92.7 %all-to-all-done.1 = bf16[32,8,16,512]{3,2,1,0:T(8,128)(2,1)} async-done(((bf16[32,8,16,512]{3,2,1,0:T(8,128)(2,1)}), bf16[32,8,16,512]{3,2,1,0:T(8,128)(2,1)}, u32[]{:S(2)}, u32[]{:S(2)}) %all-to-all-start.1) | async-done | bytes 4194336 | tf_op jit(solution)/shard_map/all_to_all | solution.py:9
  153.6 2.7 copy.94
  157.7 1.1 reshape.60
  158.7 13.0 %all_to_all.74 = bf16[8,2,4096]{2,1,0:T(2,128)(2,1)S(1)} all-to-all(bf16[8,2,4096]{2,1,0:T(2,128)(2,1)S(1)} %reshape.60), channel_id=1, replica_groups=mesh['row'=32,'col'=8] {'col'}, dimensions={0} | all-to-all | bytes 262144 | tf_op jit(solution)/shard_map/all_to_all | solution.py:51
  174.6 13.1 %all_to_all.75 = bf16[8,2,4096]{2,1,0:T(2,128)(2,1)S(1)} all-to-all(bf16[8,2,4096]{2,1,0:T(2,128)(2,1)S(1)} %reshape.62), channel_id=1, replica_groups=mesh['row'=32,'col'=8] {'col'}, dimensions={0} | all-to-all | bytes 262144 | tf_op jit(solution)/shard_map/all_to_all | solution.py:31
  188.3 4.5 convolution_bitcast_fusion
  192.8 10.4 %copy.103 = f32[512,8,512]{2,1,0:T(8,128)} copy(f32[512,8,512]{0,2,1:T(8,128)} %convolution_bitcast_fusion) | data formatting | bytes 16777216 | tf_op jit(solution)/shard_map/hij,hik->jhk/transpose | solution.py:44
  203.5 149.8 %reduce-scatter.2.cloned.1.call-done = f32[16,8,512]{2,1,0:T(8,128)} async-done(((f32[512,8,512]{2,1,0:T(8,128)}), f32[16,8,512]{2,1,0:T(8,128)}) %reduce-scatter.2.cloned.1.call-update) | async-done | bytes 262160 | tf_op jit(solution)/shard_map/reduce_scatter | solution.py:43
  353.3 1.0 convert_bitcast_fusion
  354.3 0.8 copy.104
  355.1 1.1 reshape.64
  356.2 16.0 %all_to_all.76 = bf16[8,2,4096]{2,1,0:T(2,128)(2,1)S(1)} all-to-all(bf16[8,2,4096]{2,1,0:T(2,128)(2,1)S(1)} %reshape.64), channel_id=1, replica_groups=mesh['row'=32,'col'=8] {'col'}, dimensions={0} | all-to-all | bytes 262144 | tf_op jit(solution)/shard_map/all_to_all | solution.py:52
  374.4 1.5 convolution_bitcast_fusion.1
  375.9 1.0 fusion.21
  377.0 1.3 fusion.9
  378.3 243.2 %all-reduce.2.cloned.1.call-done = f32[128,256]{1,0:T(8,128)} async-done(((f32[128,256]{1,0:T(8,128)}), f32[128,256]{1,0:T(8,128)}) %all-reduce.2.cloned.1.call-update) | async-done | bytes 131088 | tf_op jit(solution)/shard_map/psum | solution.py:66
  621.5 0.9 broadcast_multiply_fusion
  (43 shorter events, 11.9 us)
Async XLA Ops:
  7.2 19.8 %copy-start.1 = (bf16[64,16,64]{2,1,0:T(8,128)(2,1)S(1)}, bf16[64,16,64]{2,1,0:T(8,128)(2,1)}, u32[]{:S(2)}) copy-start(bf16[64,16,64]{2,1,0:T(8,128)(2,1)} %param.7) | copy-start | bytes 393220
  15.9 21.6 %all-to-all-start = ((bf16[8,2,4096]{2,1,0:T(2,128)(2,1)}), bf16[8,2,4096]{2,1,0:T(2,128)(2,1)S(1)}, u32[]{:S(2)}, u32[]{:S(2)}) async-start(bf16[8,2,4096]{2,1,0:T(2,128)(2,1)} %reshape.58), calls=%async_computation | async-start | bytes 262144 | tf_op jit(solution)/shard_map/all_to_all | solution.py:32
  37.5 13.8 %all-to-all-start.2 = ((bf16[8,2,4096]{2,1,0:T(2,128)(2,1)}), bf16[8,2,4096]{2,1,0:T(2,128)(2,1)S(1)}, u32[]{:S(2)}, u32[]{:S(2)}) async-start(bf16[8,2,4096]{2,1,0:T(2,128)(2,1)} %reshape.56), calls=%async_computation.2 | async-start | bytes 262144 | tf_op jit(solution)/shard_map/all_to_all | solution.py:30
  53.8 99.8 %all-to-all-start.1 = ((bf16[32,8,16,512]{3,2,1,0:T(8,128)(2,1)}), bf16[32,8,16,512]{3,2,1,0:T(8,128)(2,1)}, u32[]{:S(2)}, u32[]{:S(2)}) async-start(bf16[32,8,16,512]{3,2,1,0:T(8,128)(2,1)} %stack.5), calls=%async_computation.1 | async-start | bytes 8388608 | tf_op jit(solution)/shard_map/all_to_all | solution.py:9
  60.2 293.1 %reduce-scatter.2.cloned.1.call-start = ((), (), s32[]{:S(2)}) async-start(), calls=%async_computation.7 | async-start | bytes 8650752 | tf_op jit(solution)/shard_map/reduce_scatter | solution.py:43
  203.3 418.2 %all-reduce.2.cloned.1.call-start = ((), (), s32[]{:S(2)}) async-start(), calls=%async_computation.8 | async-start | bytes 262144 | tf_op jit(solution)/shard_map/psum | solution.py:66
  355.1 19.3 %copy-start = (bf16[16,64,128]{2,1,0:T(8,128)(2,1)S(1)}, bf16[16,64,128]{2,1,0:T(8,128)(2,1)}, u32[]{:S(2)}) copy-start(bf16[16,64,128]{2,1,0:T(8,128)(2,1)} %param.6) | copy-start | bytes 786436
Sparse Core Ops, SparseCore 0:
  203.4 149.8 reduce-scatter.1
  377.1 244.3 all-reduce.1
